TPU v7x, 256 devices: a whole 4x4x8 slice. The times are simulated.
256 devices in a mesh: grp: 16 (over x_lo, z), blk: 16 (over x_hi, y, core).
Axes of the slice: x: 4 (x_hi: 2, x_lo: 2; x = x_hi * 2 + x_lo), y: 4, z: 8, core: 2. Of those that a mesh axis runs over, the one named last changes fastest.
Arguments:
- raw_ints: bfloat16 [2048, 256, 512], P('grp', 'blk'), may hold values from -0.59765625 to 0.59765625
- metric: bfloat16 [2048, 2048], P(None, 'grp'), as said below
- occ_energy: float32 [256], replicated, may hold values from -2 to -0.3
- virt_energy: float32 [512], replicated, may hold values from 0.2 to 5
Outputs:
- density: float32 [2048, 256, 512], P(None, ('blk', 'grp'))
- pair_energy: float32 [256, 4], P(('blk', 'grp'))
Inputs may be any that keep to these rules, and one draw needn't show every extreme that they name: `metric`: Symmetric.
All inputs are finite; a program needn't handle non-finite values.
Results may differ from a plain program's by a relative error of at most 0.0033.
Values may be sent and summed in bfloat16 or wider, within the bound.
A program may use at most 128 MiB of HBM per device.

v0:
```python
import jax
import jax.numpy as jnp
from jax import lax
from jax.sharding import PartitionSpec as P

VISITS = 4


def swapped(value, axis, bit):
    mask = 2**bit
    pairs = [(source, source ^ mask) for source in range(lax.axis_size(axis))]
    return lax.ppermute(value, axis, pairs)


def passed_along(block, axis, distance):
    devices = range(lax.axis_size(axis))
    route = [((i - distance) % len(devices), i) for i in devices]
    return lax.ppermute(block, axis, route)


def pair_terms(own, other, e_own, e_other, virt_energy):
    coulomb = lax.dot_general(
        own, other, (((0,), (0,)), ((), ())), preferred_element_type=jnp.float32
    )
    denom = e_own + e_other - virt_energy[:, None] - virt_energy[None, :]
    amplitude = coulomb / denom
    tilde = 2.0 * amplitude - amplitude.T
    energy = jnp.sum(coulomb * tilde)
    tilde_low = tilde.astype(jnp.bfloat16)
    contrib = lax.dot_general(
        other, tilde_low, (((1,), (1,)), ((), ())), preferred_element_type=jnp.float32
    )
    return (contrib, energy)


def local(raw_ints, metric, occ_energy, virt_energy):
    n_grp = lax.axis_size("grp")
    n_blk = lax.axis_size("blk")
    total_dev = n_grp * n_blk
    moved = lax.all_to_all(raw_ints, "grp", split_axis=1, concat_axis=0, tiled=True)
    own_raw = moved.reshape(moved.shape[0], moved.shape[2])
    own = jnp.dot(
        lax.all_gather(metric, "grp", axis=1, tiled=True),
        own_raw,
        preferred_element_type=jnp.float32,
    ).astype(jnp.bfloat16)
    place = lax.axis_index("grp") * n_blk + lax.axis_index("blk")

    def orbital_at(where_at):
        return where_at % n_blk * n_grp + where_at // n_blk

    e_own = lax.dynamic_index_in_dim(occ_energy, orbital_at(place), 0, keepdims=False)
    density, energy = pair_terms(own, own, e_own, e_own, virt_energy)
    energies = [energy]
    traveller = own
    for step in range(1, VISITS):
        partner = jnp.where(
            (place - step) % 2 == 0, (place - step) % total_dev, (place + step) % total_dev
        )
        if step % 2 == 1:
            traveller = swapped(traveller, ("grp", "blk"), 0)
        else:
            shifted = passed_along(traveller, ("grp", "blk"), 1)
            paired = swapped(shifted, ("grp", "blk"), 0)
            traveller = passed_along(paired, ("grp", "blk"), -1)
        e_other = lax.dynamic_index_in_dim(occ_energy, orbital_at(partner), 0, keepdims=False)
        contrib, energy = pair_terms(own, traveller, e_own, e_other, virt_energy)
        density = density + contrib
        energies.append(energy)
    return (density[:, None, :], jnp.stack(energies)[None, :])


def solution(mesh):
    in_specs = (P("grp", "blk", None), P(None, "grp"), P(), P())
    out_specs = (P(None, ("blk", "grp"), None), P(("blk", "grp"), None))
    return jax.shard_map(local, mesh=mesh, in_specs=in_specs, out_specs=out_specs, check_vma=False)
```

profile of v0, /device:TPU:1, one launch (start us, length us, event | category | flops | bytes accessed | tf_op | source)
XLA Modules:
  0.0 311.1 jit_solution(17193218113815496922)
XLA Ops:
  7.2 0.7 all-gather.2.cloned.1.call-update
  7.9 2.8 copy.11
  10.7 71.3 %all_to_all.15 = bf16[128,16,512]{2,0,1:T(8,128)(2,1)S(1)} all-to-all(bf16[128,16,512]{2,0,1:T(8,128)(2,1)S(1)} %copy.11), channel_id=1, replica_groups=mesh['grp'=16,'blk'=16] {'grp'}, dimensions={1} | all-to-all | bytes 4194304 | tf_op jit(solution)/shard_map/all_to_all | solution.py:40
  82.0 88.1 %all-gather.2.cloned.1.call-done = bf16[2048,2048]{1,0:T(8,128)(2,1)} async-done(((bf16[2048,128]{1,0:T(8,128)(2,1)}), bf16[2048,2048]{1,0:T(8,128)(2,1)}) %all-gather.2.cloned.1.call-update) | async-done | bytes 8388624 | tf_op jit(solution)/shard_map/all_gather | solution.py:43
  170.1 8.1 %convolution_convert_fusion = bf16[2048,512]{1,0:T(8,128)(2,1)S(1)} fusion(bf16[2048,2048]{1,0:T(8,128)(2,1)} %all-gather.2.cloned.1.call-done, bf16[2048,512]{1,0:T(8,128)(2,1)S(1)} %bitcast.67), kind=kOutput, calls=%fused_computation.1 | convolution fusion | flops 4296015872 | bytes 12582912 | tf_op jit(solution)/shard_map/dot_general | solution.py:42
  178.2 1.4 copy-done.9
  179.6 6.9 %collective-permute-start = (bf16[2048,512]{1,0:T(8,128)(2,1)S(1)}, bf16[2048,512]{1,0:T(8,128)(2,1)S(1)}, u32[]{:S(2)}, u32[]{:S(2)}) collective-permute-start(bf16[2048,512]{1,0:T(8,128)(2,1)S(1)} %convolution_convert_fusion), channel_id=1, source_target_pairs={{0,1},{1,0},{2,3},{3,2},{4,5},{5,4},{6,7},{7,6},{8,9},{9,8},{10,11... | collective-permute-start | bytes 6291464 | tf_op jit(solution)/shard_map/ppermute | solution.py:12
  186.5 3.8 %collective-permute-done = bf16[2048,512]{1,0:T(8,128)(2,1)S(1)} collective-permute-done((bf16[2048,512]{1,0:T(8,128)(2,1)S(1)}, bf16[2048,512]{1,0:T(8,128)(2,1)S(1)}, u32[]{:S(2)}, u32[]{:S(2)}) %collective-permute-start) | collective-permute-done | bytes 2097184 | tf_op jit(solution)/shard_map/ppermute | solution.py:12
  190.3 1.3 copy-done.13
  191.6 1.6 collective-permute-start.1
  193.1 23.0 %collective-permute-done.1 = bf16[2048,512]{1,0:T(8,128)(2,1)S(1)} collective-permute-done((bf16[2048,512]{1,0:T(8,128)(2,1)S(1)}, bf16[2048,512]{1,0:T(8,128)(2,1)S(1)}, u32[]{:S(2)}, u32[]{:S(2)}) %collective-permute-start.1) | collective-permute-done | bytes 2097184 | tf_op jit(solution)/shard_map/ppermute | solution.py:18
  216.1 6.7 %collective-permute-start.2 = (bf16[2048,512]{1,0:T(8,128)(2,1)S(1)}, bf16[2048,512]{1,0:T(8,128)(2,1)}, u32[]{:S(2)}, u32[]{:S(2)}) collective-permute-start(bf16[2048,512]{1,0:T(8,128)(2,1)S(1)} %collective-permute-done.1), channel_id=1, source_target_pairs={{0,1},{1,0},{2,3},{3,2},{4,5},{5,4},{6,7},{7,6},{8,9},{9,8},{10,11... | collective-permute-start | bytes 6291464 | tf_op jit(solution)/shard_map/ppermute | solution.py:12
  222.8 3.9 %collective-permute-done.2 = bf16[2048,512]{1,0:T(8,128)(2,1)} collective-permute-done((bf16[2048,512]{1,0:T(8,128)(2,1)S(1)}, bf16[2048,512]{1,0:T(8,128)(2,1)}, u32[]{:S(2)}, u32[]{:S(2)}) %collective-permute-start.2) | collective-permute-done | bytes 2097184 | tf_op jit(solution)/shard_map/ppermute | solution.py:12
  226.8 0.4 collective-permute-start.3
  227.1 0.6 fusion.15
  232.4 3.5 %fusion.16 = f32[512,512]{1,0:T(8,128)S(1)} fusion(bf16[2048,512]{1,0:T(8,128)(2,1)} %copy-done.9), kind=kOutput, calls=%fused_computation.27 | convolution fusion | flops 1073741824 | bytes 3145728 | tf_op jit(solution)/shard_map/dot_general | solution.py:22
  235.9 0.3 copy.12
  236.2 16.3 %collective-permute-done.3 = bf16[2048,512]{1,0:T(8,128)(2,1)} collective-permute-done((bf16[2048,512]{1,0:T(8,128)(2,1)}, bf16[2048,512]{1,0:T(8,128)(2,1)}, u32[]{:S(2)}, u32[]{:S(2)}) %collective-permute-start.3) | collective-permute-done | bytes 2097184 | tf_op jit(solution)/shard_map/ppermute | solution.py:18
  252.7 5.3 %fusion.9 = f32[2048,512]{1,0:T(8,128)} fusion(bf16[2048,512]{1,0:T(8,128)(2,1)} %copy-done.9, f32[512,512]{0,1:T(8,128)S(1)} %copy.12, f32[512,512]{1,0:T(8,128)S(1)} %fusion.16, f32[512]{0:T(512)S(1)} %copy-done.7, f32[512]{0:T(512)S(1)} %get-tuple-element.12), kind=kOutput, calls=%fused_computation.19 | convolution fusion | flops 1075576832 | bytes 8392704 | tf_op jit(solution)/shard_map/dot_general | solution.py:30
  258.1 1.3 fusion.17
  259.3 0.3 copy.13
  259.7 5.6 %fusion.7 = f32[2048,512]{1,0:T(8,128)} fusion(bf16[2048,512]{1,0:T(8,128)(2,1)} %copy-done.13, f32[512,512]{0,1:T(8,128)S(1)} %copy.13, f32[512,512]{1,0:T(8,128)S(1)} %fusion.17, f32[512]{0:T(512)S(1)} %get-tuple-element.11, f32[512]{0:T(512)S(1)} %copy-done.7), kind=kOutput, calls=%fused_computation.17 | convolution fusion | flops 1075576832 | bytes 8392704 | tf_op jit(solution)/shard_map/dot_general | solution.py:30
  265.3 3.9 %fusion.18 = f32[512,512]{1,0:T(8,128)} fusion(bf16[2048,512]{1,0:T(8,128)(2,1)S(1)} %copy-done.11, bf16[2048,512]{1,0:T(8,128)(2,1)} %collective-permute-done.3), kind=kOutput, calls=%fused_computation.29 | convolution fusion | flops 1073741824 | bytes 5242880 | tf_op jit(solution)/shard_map/dot_general | solution.py:22
  269.2 1.6 copy.14
  270.9 5.6 %fusion.5 = f32[2048,512]{1,0:T(8,128)} fusion(bf16[2048,512]{1,0:T(8,128)(2,1)} %collective-permute-done.3, f32[512,512]{0,1:T(8,128)S(1)} %copy.14, f32[512,512]{1,0:T(8,128)S(1)} %copy-done.5, f32[512]{0:T(512)S(1)} %get-tuple-element.13, f32[512]{0:T(512)S(1)} %copy-done.7), kind=kOutput, calls=%fused_computation.15 | convolution fusion | flops 1075576832 | bytes 8392704 | tf_op jit(solution)/shard_map/dot_general | solution.py:30
  276.5 2.9 fusion.19
  279.4 0.3 copy.15
  279.7 4.4 %multiply_reduce_fusion.3 = (f32[]{:T(128)}, f32[]{:T(128)}, f32[]{:T(128)}, f32[]{:T(128)}) fusion(f32[512,512]{1,0:T(8,128)S(1)} %fusion.16, f32[512]{0:T(512)S(1)} %copy-done.7, f32[512]{0:T(512)S(1)} %get-tuple-element.12, f32[512,512]{0,1:T(8,128)} %copy-done.2, f32[512,512]{1,0:T(8,128)S(1)} %fusion.19, f32[512]{0:T(512)S(1)} %get-tuple-element.10, ...), kind=kLoop, calls=%fused_computation.13 | loop fusion | flops 8388604 | bytes 8398864 | tf_op jit(solution)/shard_map/reduce_sum | solution.py:28
  284.2 0.6 copy-done.1
  284.8 4.9 %add_bitcast_fusion = f32[2048,1,512]{2,0,1:T(8,128)S(1)} fusion(f32[2048,512]{1,0:T(8,128)} %fusion.5, f32[2048,512]{1,0:T(8,128)S(1)} %copy-done, f32[2048,512]{1,0:T(8,128)S(1)} %copy-done.1, bf16[2048,512]{1,0:T(8,128)(2,1)} %collective-permute-done.4, f32[512,512]{0,1:T(8,128)S(1)} %copy.15, f32[512,512]{1,0:T(8,128)S(1)} %fusion.19, ...), kind=kOutput, calls=%fused_computation | convolution fusion | flops 1078722560 | bytes 20975616 | tf_op jit(solution)/shard_map/dot_general | solution.py:30
  289.7 11.7 %copy.16 = f32[2048,1,512]{2,1,0:T(1,128)} copy(f32[2048,1,512]{2,0,1:T(8,128)S(1)} %add_bitcast_fusion) | data formatting | bytes 8388608
  301.4 2.9 maximum_bitcast_fusion
  (31 shorter events, 0.3 us)
Async XLA Ops:
  7.2 162.9 %all-gather.2.cloned.1.call-start = ((), (), s32[]{:S(2)}) async-start(), calls=%async_computation.1 | async-start | bytes 8912896 | tf_op jit(solution)/shard_map/all_gather | solution.py:43
  170.1 57.0 %copy-start.8 = (f32[256]{0:T(256)S(1)}, f32[256]{0:T(256)}, u32[]{:S(2)}) copy-start(f32[256]{0:T(256)} %param.6) | copy-start | bytes 3076
  170.1 62.3 %copy-start.7 = (f32[512]{0:T(512)S(1)}, f32[512]{0:T(512)}, u32[]{:S(2)}) copy-start(f32[512]{0:T(512)} %param.7) | copy-start | bytes 6148
  178.2 1.4 copy-start.9
  179.6 10.6 %collective-permute-start = (bf16[2048,512]{1,0:T(8,128)(2,1)S(1)}, bf16[2048,512]{1,0:T(8,128)(2,1)S(1)}, u32[]{:S(2)}, u32[]{:S(2)}) collective-permute-start(bf16[2048,512]{1,0:T(8,128)(2,1)S(1)} %convolution_convert_fusion), channel_id=1, source_target_pairs={{0,1},{1,0},{2,3},{3,2},{4,5},{5,4},{6,7},{7,6},{8,9},{9,8},{10,11... | collective-permute-start | bytes 6291464 | tf_op jit(solution)/shard_map/ppermute | solution.py:12
  190.3 1.3 copy-start.13
  191.6 24.5 %collective-permute-start.1 = (bf16[2048,512]{1,0:T(8,128)(2,1)S(1)}, bf16[2048,512]{1,0:T(8,128)(2,1)S(1)}, u32[]{:S(2)}, u32[]{:S(2)}) collective-permute-start(bf16[2048,512]{1,0:T(8,128)(2,1)S(1)} %collective-permute-done), channel_id=1, source_target_pairs={{255,0},{0,1},{1,2},{2,3},{3,4},{4,5},{5,6},{6,7},{7,8},{8,9},{9,1... | collective-permute-start | bytes 6291464 | tf_op jit(solution)/shard_map/ppermute | solution.py:18
  216.1 10.6 %collective-permute-start.2 = (bf16[2048,512]{1,0:T(8,128)(2,1)S(1)}, bf16[2048,512]{1,0:T(8,128)(2,1)}, u32[]{:S(2)}, u32[]{:S(2)}) collective-permute-start(bf16[2048,512]{1,0:T(8,128)(2,1)S(1)} %collective-permute-done.1), channel_id=1, source_target_pairs={{0,1},{1,0},{2,3},{3,2},{4,5},{5,4},{6,7},{7,6},{8,9},{9,8},{10,11... | collective-permute-start | bytes 6291464 | tf_op jit(solution)/shard_map/ppermute | solution.py:12
  226.8 25.8 %collective-permute-start.3 = (bf16[2048,512]{1,0:T(8,128)(2,1)}, bf16[2048,512]{1,0:T(8,128)(2,1)}, u32[]{:S(2)}, u32[]{:S(2)}) collective-permute-start(bf16[2048,512]{1,0:T(8,128)(2,1)} %collective-permute-done.2), channel_id=1, source_target_pairs={{1,0},{2,1},{3,2},{4,3},{5,4},{6,5},{7,6},{8,7},{9,8},{10,9},{11,1... | collective-permute-start | bytes 6291464 | tf_op jit(solution)/shard_map/ppermute | solution.py:18
  236.2 21.8 %copy-start.2 = (f32[512,512]{0,1:T(8,128)}, f32[512,512]{0,1:T(8,128)S(1)}, u32[]{:S(2)}) copy-start(f32[512,512]{0,1:T(8,128)S(1)} %copy.12) | copy-start | bytes 3145732
  252.5 24.0 %collective-permute-start.4 = (bf16[2048,512]{1,0:T(8,128)(2,1)}, bf16[2048,512]{1,0:T(8,128)(2,1)}, u32[]{:S(2)}, u32[]{:S(2)}) collective-permute-start(bf16[2048,512]{1,0:T(8,128)(2,1)} %collective-permute-done.3), channel_id=1, source_target_pairs={{0,1},{1,0},{2,3},{3,2},{4,5},{5,4},{6,7},{7,6},{8,9},{9,8},{10,11... | collective-permute-start | bytes 6291464 | tf_op jit(solution)/shard_map/ppermute | solution.py:12
  252.7 5.3 %copy-start.10 = (bf16[2048,512]{1,0:T(8,128)(2,1)S(1)}, bf16[2048,512]{1,0:T(8,128)(2,1)}, u32[]{:S(2)}) copy-start(bf16[2048,512]{1,0:T(8,128)(2,1)} %copy-done.9) | copy-start | bytes 6291460
  252.7 5.3 %copy-start.14 = (bf16[2048,512]{1,0:T(8,128)(2,1)S(1)}, bf16[2048,512]{1,0:T(8,128)(2,1)}, u32[]{:S(2)}) copy-start(bf16[2048,512]{1,0:T(8,128)(2,1)} %copy-done.13) | copy-start | bytes 6291460
  259.3 6.0 %copy-start.3 = (f32[512,512]{1,0:T(8,128)}, f32[512,512]{1,0:T(8,128)S(1)}, u32[]{:S(2)}) copy-start(f32[512,512]{1,0:T(8,128)S(1)} %fusion.17) | copy-start | bytes 3145732
  259.7 5.6 %copy-start.4 = (f32[512,512]{0,1:T(8,128)}, f32[512,512]{0,1:T(8,128)S(1)}, u32[]{:S(2)}) copy-start(f32[512,512]{0,1:T(8,128)S(1)} %copy.13) | copy-start | bytes 3145732
  259.7 5.6 %copy-start.11 = (bf16[2048,512]{1,0:T(8,128)(2,1)S(1)}, bf16[2048,512]{1,0:T(8,128)(2,1)}, u32[]{:S(2)}) copy-start(bf16[2048,512]{1,0:T(8,128)(2,1)} %copy-done.9) | copy-start | bytes 6291460
  269.2 1.7 copy-start.5
  270.8 5.7 %copy-start.6 = (f32[512,512]{0,1:T(8,128)}, f32[512,512]{0,1:T(8,128)S(1)}, u32[]{:S(2)}) copy-start(f32[512,512]{0,1:T(8,128)S(1)} %copy.14) | copy-start | bytes 3145732
  270.9 5.7 %copy-start.12 = (bf16[2048,512]{1,0:T(8,128)(2,1)S(1)}, bf16[2048,512]{1,0:T(8,128)(2,1)}, u32[]{:S(2)}) copy-start(bf16[2048,512]{1,0:T(8,128)(2,1)} %copy-done.9) | copy-start | bytes 6291460
  279.7 4.4 %copy-start = (f32[2048,512]{1,0:T(8,128)S(1)}, f32[2048,512]{1,0:T(8,128)}, u32[]{:S(2)}) copy-start(f32[2048,512]{1,0:T(8,128)} %fusion.9) | copy-start | bytes 12582916
  279.7 5.0 %copy-start.1 = (f32[2048,512]{1,0:T(8,128)S(1)}, f32[2048,512]{1,0:T(8,128)}, u32[]{:S(2)}) copy-start(f32[2048,512]{1,0:T(8,128)} %fusion.7) | copy-start | bytes 12582916
Sparse Core Ops, SparseCore 0:
  9.7 160.3 all-gather.1
where the time goes:
time: 312 us; the launch traced here: 311 us
  waiting for transfers between devices  136 us (44%)
  blocking collectives  71.3 us (23%)
  matrix products  41.1 us (13%)
  local copies, waits for them, and re-layouts  21 us (7%)
  between operations  18.8 us (6%)
  starting transfers between devices  15.8 us (5%)
  other arithmetic  7.37 us (2%)
    all_gather x1, waiting for transfers between devices, local(): lax.all_gather(metric, 'grp', axis=1, tiled=True)  88.1 us
    all_to_all x1, blocking collectives, local(): lax.all_to_all(raw_ints, 'grp', split_axis=1, concat_axis=0, tiled=True)  71.3 us
    ppermute x2, waiting for transfers between devices, passed_along(): return lax.ppermute(block, axis, route)  39.3 us
    dot_general x4, matrix products, pair_terms(): lax.dot_general(other, tilde_low, (((1,), (1,)), ((), ())), preferred_ele...  21.5 us
    unnamed x32, local copies, waits for them, and re-layouts  17.8 us
    ppermute x3, starting transfers between devices, swapped(): return lax.ppermute(value, axis, pairs)  13.8 us
    dot_general x4, matrix products, pair_terms(): lax.dot_general(own, other, (((0,), (0,)), ((), ())), preferred_element_t...  11.5 us
    dot_general x1, matrix products, local(): jnp.dot(lax.all_gather(metric, 'grp', axis=1, tiled=True), own_raw, prefe...  8.13 us
  transfers between devices with their start and end apart: 6, of which 5 were waited for; matrix products, arithmetic and copies ran while one was open for 10% of the time, Pallas kernels for 0%

commit v1 on v0

--- a/solution.py
+++ b/solution.py
@@ -2,8 +2,15 @@
 import jax.numpy as jnp
 from jax import lax
 from jax.sharding import PartitionSpec as P
+from jax.lax import all_to_all, axis_size
 
 VISITS = 4
+use_ladders_now = lambda chunk, dim_no: jnp.concatenate(
+    all_to_all(
+        jnp.stack(axis_size("grp") * [chunk], 0), axis_name="grp", split_axis=0, concat_axis=0
+    ),
+    dim_no,
+)
 
 
 def swapped(value, axis, bit):
@@ -39,11 +46,9 @@
     total_dev = n_grp * n_blk
     moved = lax.all_to_all(raw_ints, "grp", split_axis=1, concat_axis=0, tiled=True)
     own_raw = moved.reshape(moved.shape[0], moved.shape[2])
-    own = jnp.dot(
-        lax.all_gather(metric, "grp", axis=1, tiled=True),
-        own_raw,
-        preferred_element_type=jnp.float32,
-    ).astype(jnp.bfloat16)
+    own = jnp.dot(use_ladders_now(metric, 1), own_raw, preferred_element_type=jnp.float32).astype(
+        jnp.bfloat16
+    )
     place = lax.axis_index("grp") * n_blk + lax.axis_index("blk")
 
     def orbital_at(where_at):

time: 312 us -> 378 us (1.21)
  blocking collectives: 71.3 us -> 189 us
  waiting for transfers between devices: 136 us -> 94.4 us
  between operations: 18.8 us -> 5.46 us
  starting transfers between devices: 15.8 us -> 22 us
    all_to_all x1, blocking collectives: 71.3 us -> 189 us  [all_to_all(jnp.stack(axis_size('grp') * [chunk], 0), axis_name='grp', spl...]
    all_gather x1 -> x0, waiting for transfers between devices: 88.1 us -> none  [local(): lax.all_gather(metric, 'grp', axis=1, tiled=True)]
    all_to_all x0 -> x1, waiting for transfers between devices: none -> 47.4 us  [local(): lax.all_to_all(raw_ints, 'grp', split_axis=1, concat_axis=0, tiled=True)]
    all_to_all x0 -> x1, starting transfers between devices: none -> 10.2 us  [local(): lax.all_to_all(raw_ints, 'grp', split_axis=1, concat_axis=0, tiled=True)]
    ppermute x3, starting transfers between devices: 13.8 us -> 9.88 us  [swapped(): return lax.ppermute(value, axis, pairs)]
    unnamed x32 -> x35, local copies, waits for them, and re-layouts: 17.8 us -> 18 us
  transfers between devices with their start and end apart: 6 -> 6, of which waited for: 5 -> 5; matrix products, arithmetic and copies ran while one was open for 10% -> 7% of each run, Pallas kernels for 0% -> 0%
where the time goes in v1:
time: 378 us
  blocking collectives  189 us (50%)
  waiting for transfers between devices  94.4 us (25%)
  matrix products  37.7 us (10%)
  local copies, waits for them, and re-layouts  22.3 us (6%)
  starting transfers between devices  22 us (6%)
  other arithmetic  7.37 us (2%)
  between operations  5.46 us (1%)
    all_to_all x1, blocking collectives, all_to_all(jnp.stack(axis_size('grp') * [chunk], 0), axis_name='grp', spl...  189 us
    all_to_all x1, waiting for transfers between devices, local(): lax.all_to_all(raw_ints, 'grp', split_axis=1, concat_axis=0, tiled=True)  47.4 us
    ppermute x2, waiting for transfers between devices, passed_along(): return lax.ppermute(block, axis, route)  39.3 us
    dot_general x4, matrix products, pair_terms(): lax.dot_general(other, tilde_low, (((1,), (1,)), ((), ())), preferred_ele...  21.5 us
    unnamed x35, local copies, waits for them, and re-layouts  18 us
    dot_general x4, matrix products, pair_terms(): lax.dot_general(own, other, (((0,), (0,)), ((), ())), preferred_element_t...  11.5 us
    all_to_all x1, starting transfers between devices, local(): lax.all_to_all(raw_ints, 'grp', split_axis=1, concat_axis=0, tiled=True)  10.2 us
    ppermute x3, starting transfers between devices, swapped(): return lax.ppermute(value, axis, pairs)  9.88 us
  transfers between devices with their start and end apart: 6, of which 5 were waited for; matrix products, arithmetic and copies ran while one was open for 7% of the time, Pallas kernels for 0%

profile of v1, /device:TPU:1, one launch (start us, length us, event | category | flops | bytes accessed | tf_op | source)
XLA Modules:
  0.0 378.0 jit_solution(17965066926041343334)
XLA Ops:
  0.6 4.1 %copy.12 = bf16[128,16,512]{2,0,1:T(8,128)(2,1)} copy(bf16[128,16,512]{2,1,0:T(8,128)(2,1)} %param.4) | data formatting | bytes 4194304 | tf_op args[0]
  4.7 10.2 %all-to-all-start.1 = ((bf16[128,16,512]{2,0,1:T(8,128)(2,1)}), bf16[128,16,512]{2,0,1:T(8,128)(2,1)S(1)}, u32[]{:S(2)}, u32[]{:S(2)}) async-start(bf16[128,16,512]{2,0,1:T(8,128)(2,1)} %copy.12), calls=%async_computation.1 | async-start | bytes 4194304 | tf_op jit(solution)/shard_map/all_to_all | solution.py:47
  15.1 47.4 %all-to-all-done.1 = bf16[128,16,512]{2,0,1:T(8,128)(2,1)S(1)} async-done(((bf16[128,16,512]{2,0,1:T(8,128)(2,1)}), bf16[128,16,512]{2,0,1:T(8,128)(2,1)S(1)}, u32[]{:S(2)}, u32[]{:S(2)}) %all-to-all-start.1) | async-done | bytes 2097184 | tf_op jit(solution)/shard_map/all_to_all | solution.py:47
  62.5 1.1 stack.12
  63.6 188.7 %all_to_all.20 = bf16[16,2048,128]{1,2,0:T(8,128)(2,1)S(1)} all-to-all(bf16[16,2048,128]{1,2,0:T(8,128)(2,1)S(1)} %stack.12), channel_id=1, replica_groups=mesh['grp'=16,'blk'=16] {'grp'}, dimensions={0} | all-to-all | bytes 16777216 | tf_op jit(solution)/shard_map/all_to_all | solution.py:9
  252.3 4.8 %convolution_convert_fusion = bf16[2048,512]{1,0:T(8,128)(2,1)S(1)} fusion(bf16[2048,2048]{0,1:T(8,128)(2,1)S(1)} %bitcast.70, bf16[2048,512]{1,0:T(8,128)(2,1)S(1)} %bitcast.71), kind=kOutput, calls=%fused_computation.1 | convolution fusion | flops 4296015872 | bytes 12582912 | tf_op jit(solution)/shard_map/dot_general | solution.py:49
  257.1 1.4 copy-done.10
  258.5 3.2 collective-permute-start
  261.6 3.8 %collective-permute-done = bf16[2048,512]{1,0:T(8,128)(2,1)S(1)} collective-permute-done((bf16[2048,512]{1,0:T(8,128)(2,1)S(1)}, bf16[2048,512]{1,0:T(8,128)(2,1)S(1)}, u32[]{:S(2)}, u32[]{:S(2)}) %collective-permute-start) | collective-permute-done | bytes 2097184 | tf_op jit(solution)/shard_map/ppermute | solution.py:19
  265.4 1.6 collective-permute-start.1
  267.0 23.0 %collective-permute-done.1 = bf16[2048,512]{1,0:T(8,128)(2,1)S(1)} collective-permute-done((bf16[2048,512]{1,0:T(8,128)(2,1)S(1)}, bf16[2048,512]{1,0:T(8,128)(2,1)S(1)}, u32[]{:S(2)}, u32[]{:S(2)}) %collective-permute-start.1) | collective-permute-done | bytes 2097184 | tf_op jit(solution)/shard_map/ppermute | solution.py:25
  290.0 6.7 %collective-permute-start.2 = (bf16[2048,512]{1,0:T(8,128)(2,1)S(1)}, bf16[2048,512]{1,0:T(8,128)(2,1)}, u32[]{:S(2)}, u32[]{:S(2)}) collective-permute-start(bf16[2048,512]{1,0:T(8,128)(2,1)S(1)} %collective-permute-done.1), channel_id=1, source_target_pairs={{0,1},{1,0},{2,3},{3,2},{4,5},{5,4},{6,7},{7,6},{8,9},{9,8},{10,11... | collective-permute-start | bytes 6291464 | tf_op jit(solution)/shard_map/ppermute | solution.py:19
  296.7 3.9 %collective-permute-done.2 = bf16[2048,512]{1,0:T(8,128)(2,1)} collective-permute-done((bf16[2048,512]{1,0:T(8,128)(2,1)S(1)}, bf16[2048,512]{1,0:T(8,128)(2,1)}, u32[]{:S(2)}, u32[]{:S(2)}) %collective-permute-start.2) | collective-permute-done | bytes 2097184 | tf_op jit(solution)/shard_map/ppermute | solution.py:19
  300.6 0.4 collective-permute-start.3
  301.0 0.6 fusion.15
  306.2 3.5 fusion.16
  309.7 0.3 copy.13
  310.1 16.3 %collective-permute-done.3 = bf16[2048,512]{1,0:T(8,128)(2,1)} collective-permute-done((bf16[2048,512]{1,0:T(8,128)(2,1)}, bf16[2048,512]{1,0:T(8,128)(2,1)}, u32[]{:S(2)}, u32[]{:S(2)}) %collective-permute-start.3) | collective-permute-done | bytes 2097184 | tf_op jit(solution)/shard_map/ppermute | solution.py:25
  326.4 5.3 %fusion.9 = f32[2048,512]{1,0:T(8,128)} fusion(bf16[2048,512]{1,0:T(8,128)(2,1)} %copy-done.10, f32[512,512]{0,1:T(8,128)S(1)} %copy.13, f32[512,512]{1,0:T(8,128)S(1)} %fusion.16, f32[512]{0:T(512)S(1)} %copy-done.8, f32[512]{0:T(512)S(1)} %get-tuple-element.12), kind=kOutput, calls=%fused_computation.19 | convolution fusion | flops 1075576832 | bytes 8392704 | tf_op jit(solution)/shard_map/dot_general | solution.py:37
  331.7 1.3 fusion.17
  333.0 0.3 copy.14
  333.4 5.6 %fusion.7 = f32[2048,512]{1,0:T(8,128)} fusion(bf16[2048,512]{1,0:T(8,128)(2,1)} %copy-done.14, f32[512,512]{0,1:T(8,128)S(1)} %copy.14, f32[512,512]{1,0:T(8,128)S(1)} %fusion.17, f32[512]{0:T(512)S(1)} %get-tuple-element.11, f32[512]{0:T(512)S(1)} %copy-done.8), kind=kOutput, calls=%fused_computation.17 | convolution fusion | flops 1075576832 | bytes 8392704 | tf_op jit(solution)/shard_map/dot_general | solution.py:37
  339.0 3.9 %fusion.18 = f32[512,512]{1,0:T(8,128)} fusion(bf16[2048,512]{1,0:T(8,128)(2,1)S(1)} %copy-done.12, bf16[2048,512]{1,0:T(8,128)(2,1)} %collective-permute-done.3), kind=kOutput, calls=%fused_computation.29 | convolution fusion | flops 1073741824 | bytes 5242880 | tf_op jit(solution)/shard_map/dot_general | solution.py:29
  342.8 1.6 copy.15
  344.5 5.6 %fusion.5 = f32[2048,512]{1,0:T(8,128)} fusion(bf16[2048,512]{1,0:T(8,128)(2,1)} %collective-permute-done.3, f32[512,512]{0,1:T(8,128)S(1)} %copy.15, f32[512,512]{1,0:T(8,128)S(1)} %copy-done.5, f32[512]{0:T(512)S(1)} %get-tuple-element.13, f32[512]{0:T(512)S(1)} %copy-done.8), kind=kOutput, calls=%fused_computation.15 | convolution fusion | flops 1075576832 | bytes 8392704 | tf_op jit(solution)/shard_map/dot_general | solution.py:37
  350.2 2.9 fusion.19
  353.0 0.3 copy.16
  353.4 4.4 %multiply_reduce_fusion.3 = (f32[]{:T(128)}, f32[]{:T(128)}, f32[]{:T(128)}, f32[]{:T(128)}) fusion(f32[512,512]{1,0:T(8,128)S(1)} %fusion.16, f32[512]{0:T(512)S(1)} %copy-done.8, f32[512]{0:T(512)S(1)} %get-tuple-element.12, f32[512,512]{0,1:T(8,128)} %copy-done.2, f32[512,512]{1,0:T(8,128)S(1)} %fusion.19, f32[512]{0:T(512)S(1)} %get-tuple-element.10, ...), kind=kLoop, calls=%fused_computation.13 | loop fusion | flops 8388604 | bytes 8398864 | tf_op jit(solution)/shard_map/reduce_sum | solution.py:35
  357.8 0.6 copy-done.1
  358.4 4.9 %add_bitcast_fusion = f32[2048,1,512]{2,0,1:T(8,128)S(1)} fusion(f32[2048,512]{1,0:T(8,128)} %fusion.5, f32[2048,512]{1,0:T(8,128)S(1)} %copy-done, f32[2048,512]{1,0:T(8,128)S(1)} %copy-done.1, bf16[2048,512]{1,0:T(8,128)(2,1)} %collective-permute-done.4, f32[512,512]{0,1:T(8,128)S(1)} %copy.16, f32[512,512]{1,0:T(8,128)S(1)} %fusion.19, ...), kind=kOutput, calls=%fused_computation | convolution fusion | flops 1078722560 | bytes 20975616 | tf_op jit(solution)/shard_map/dot_general | solution.py:37
  363.3 11.7 %copy.17 = f32[2048,1,512]{2,1,0:T(1,128)} copy(f32[2048,1,512]{2,0,1:T(8,128)S(1)} %add_bitcast_fusion) | data formatting | bytes 8388608
  375.0 2.9 maximum_bitcast_fusion
  (34 shorter events, 0.3 us)
Async XLA Ops:
  4.7 10.2 %copy-start.7 = (bf16[2048,128]{1,0:T(8,128)(2,1)S(1)}, bf16[2048,128]{1,0:T(8,128)(2,1)}, u32[]{:S(2)}) copy-start(bf16[2048,128]{1,0:T(8,128)(2,1)} %param.5) | copy-start | bytes 1572868
  4.7 57.8 %all-to-all-start.1 = ((bf16[128,16,512]{2,0,1:T(8,128)(2,1)}), bf16[128,16,512]{2,0,1:T(8,128)(2,1)S(1)}, u32[]{:S(2)}, u32[]{:S(2)}) async-start(bf16[128,16,512]{2,0,1:T(8,128)(2,1)} %copy.12), calls=%async_computation.1 | async-start | bytes 4194304 | tf_op jit(solution)/shard_map/all_to_all | solution.py:47
  252.3 48.7 %copy-start.9 = (f32[256]{0:T(256)S(1)}, f32[256]{0:T(256)}, u32[]{:S(2)}) copy-start(f32[256]{0:T(256)} %param.6) | copy-start | bytes 3076
  252.3 53.9 %copy-start.8 = (f32[512]{0:T(512)S(1)}, f32[512]{0:T(512)}, u32[]{:S(2)}) copy-start(f32[512]{0:T(512)} %param.7) | copy-start | bytes 6148
  257.1 1.4 copy-start.10
  258.5 6.9 %collective-permute-start = (bf16[2048,512]{1,0:T(8,128)(2,1)S(1)}, bf16[2048,512]{1,0:T(8,128)(2,1)S(1)}, u32[]{:S(2)}, u32[]{:S(2)}) collective-permute-start(bf16[2048,512]{1,0:T(8,128)(2,1)S(1)} %convolution_convert_fusion), channel_id=1, source_target_pairs={{0,1},{1,0},{2,3},{3,2},{4,5},{5,4},{6,7},{7,6},{8,9},{9,8},{10,11... | collective-permute-start | bytes 6291464 | tf_op jit(solution)/shard_map/ppermute | solution.py:19
  265.4 40.8 %copy-start.14 = (bf16[2048,512]{1,0:T(8,128)(2,1)}, bf16[2048,512]{1,0:T(8,128)(2,1)S(1)}, u32[]{:S(2)}) copy-start(bf16[2048,512]{1,0:T(8,128)(2,1)S(1)} %collective-permute-done) | copy-start | bytes 6291460
  265.4 24.5 %collective-permute-start.1 = (bf16[2048,512]{1,0:T(8,128)(2,1)S(1)}, bf16[2048,512]{1,0:T(8,128)(2,1)S(1)}, u32[]{:S(2)}, u32[]{:S(2)}) collective-permute-start(bf16[2048,512]{1,0:T(8,128)(2,1)S(1)} %collective-permute-done), channel_id=1, source_target_pairs={{255,0},{0,1},{1,2},{2,3},{3,4},{4,5},{5,6},{6,7},{7,8},{8,9},{9,1... | collective-permute-start | bytes 6291464 | tf_op jit(solution)/shard_map/ppermute | solution.py:25
  290.0 10.6 %collective-permute-start.2 = (bf16[2048,512]{1,0:T(8,128)(2,1)S(1)}, bf16[2048,512]{1,0:T(8,128)(2,1)}, u32[]{:S(2)}, u32[]{:S(2)}) collective-permute-start(bf16[2048,512]{1,0:T(8,128)(2,1)S(1)} %collective-permute-done.1), channel_id=1, source_target_pairs={{0,1},{1,0},{2,3},{3,2},{4,5},{5,4},{6,7},{7,6},{8,9},{9,8},{10,11... | collective-permute-start | bytes 6291464 | tf_op jit(solution)/shard_map/ppermute | solution.py:19
  300.6 25.8 %collective-permute-start.3 = (bf16[2048,512]{1,0:T(8,128)(2,1)}, bf16[2048,512]{1,0:T(8,128)(2,1)}, u32[]{:S(2)}, u32[]{:S(2)}) collective-permute-start(bf16[2048,512]{1,0:T(8,128)(2,1)} %collective-permute-done.2), channel_id=1, source_target_pairs={{1,0},{2,1},{3,2},{4,3},{5,4},{6,5},{7,6},{8,7},{9,8},{10,9},{11,1... | collective-permute-start | bytes 6291464 | tf_op jit(solution)/shard_map/ppermute | solution.py:25
  310.1 21.6 %copy-start.2 = (f32[512,512]{0,1:T(8,128)}, f32[512,512]{0,1:T(8,128)S(1)}, u32[]{:S(2)}) copy-start(f32[512,512]{0,1:T(8,128)S(1)} %copy.13) | copy-start | bytes 3145732
  326.4 23.8 %collective-permute-start.4 = (bf16[2048,512]{1,0:T(8,128)(2,1)}, bf16[2048,512]{1,0:T(8,128)(2,1)}, u32[]{:S(2)}, u32[]{:S(2)}) collective-permute-start(bf16[2048,512]{1,0:T(8,128)(2,1)} %collective-permute-done.3), channel_id=1, source_target_pairs={{0,1},{1,0},{2,3},{3,2},{4,5},{5,4},{6,7},{7,6},{8,9},{9,8},{10,11... | collective-permute-start | bytes 6291464 | tf_op jit(solution)/shard_map/ppermute | solution.py:19
  326.4 5.3 %copy-start.11 = (bf16[2048,512]{1,0:T(8,128)(2,1)S(1)}, bf16[2048,512]{1,0:T(8,128)(2,1)}, u32[]{:S(2)}) copy-start(bf16[2048,512]{1,0:T(8,128)(2,1)} %copy-done.10) | copy-start | bytes 6291460
  326.4 5.3 %copy-start.15 = (bf16[2048,512]{1,0:T(8,128)(2,1)S(1)}, bf16[2048,512]{1,0:T(8,128)(2,1)}, u32[]{:S(2)}) copy-start(bf16[2048,512]{1,0:T(8,128)(2,1)} %copy-done.14) | copy-start | bytes 6291460
  333.0 6.0 %copy-start.3 = (f32[512,512]{1,0:T(8,128)}, f32[512,512]{1,0:T(8,128)S(1)}, u32[]{:S(2)}) copy-start(f32[512,512]{1,0:T(8,128)S(1)} %fusion.17) | copy-start | bytes 3145732
  333.3 5.6 %copy-start.4 = (f32[512,512]{0,1:T(8,128)}, f32[512,512]{0,1:T(8,128)S(1)}, u32[]{:S(2)}) copy-start(f32[512,512]{0,1:T(8,128)S(1)} %copy.14) | copy-start | bytes 3145732
  333.4 5.6 %copy-start.12 = (bf16[2048,512]{1,0:T(8,128)(2,1)S(1)}, bf16[2048,512]{1,0:T(8,128)(2,1)}, u32[]{:S(2)}) copy-start(bf16[2048,512]{1,0:T(8,128)(2,1)} %copy-done.10) | copy-start | bytes 6291460
  342.8 1.7 copy-start.5
  344.5 5.7 %copy-start.6 = (f32[512,512]{0,1:T(8,128)}, f32[512,512]{0,1:T(8,128)S(1)}, u32[]{:S(2)}) copy-start(f32[512,512]{0,1:T(8,128)S(1)} %copy.15) | copy-start | bytes 3145732
  344.5 5.7 %copy-start.13 = (bf16[2048,512]{1,0:T(8,128)(2,1)S(1)}, bf16[2048,512]{1,0:T(8,128)(2,1)}, u32[]{:S(2)}) copy-start(bf16[2048,512]{1,0:T(8,128)(2,1)} %copy-done.10) | copy-start | bytes 6291460
  353.4 4.4 %copy-start = (f32[2048,512]{1,0:T(8,128)S(1)}, f32[2048,512]{1,0:T(8,128)}, u32[]{:S(2)}) copy-start(f32[2048,512]{1,0:T(8,128)} %fusion.9) | copy-start | bytes 12582916
  353.4 5.0 %copy-start.1 = (f32[2048,512]{1,0:T(8,128)S(1)}, f32[2048,512]{1,0:T(8,128)}, u32[]{:S(2)}) copy-start(f32[2048,512]{1,0:T(8,128)} %fusion.7) | copy-start | bytes 12582916
